TPU v7x, 32 devices: a whole 2x2x4 slice. The times are simulated.
32 devices in a mesh: pts: 16 (over z, x, core), proto: 2 (over y).
Axes of the slice: x: 2, y: 2, z: 4, core: 2. Of those that a mesh axis runs over, the one named last changes fastest.
Arguments:
- points: bfloat16 [128, 128, 1024], P('pts', None, 'proto'), as said below
- prototypes: bfloat16 [32, 512, 1024], P(('pts', 'proto')), as said below
- coarse_duals: float32 [32, 512], P(('pts', 'proto')), may hold values from -8 to 8
- active: int32 [128, 8], P('pts'), may hold values from 0 to 31, as said below
Outputs:
- point_duals: float32 [128, 128], P('pts')
- new_duals: float32 [32, 512], P(('pts', 'proto'))
Inputs may be any that keep to these rules, and one draw needn't show every extreme that they name: `active`: each row names 8 different blocks. Block b belongs to owner group b // 2. The 8 rows of one index of pts name any one owner group at most 8 times, and exactly that often for 8 groups. Over all rows every owner group is named 64 times in all, every block at least once and at most 32 times, and in every owner group some block exactly 32 times. `points`: Real-valued embeddings. `prototypes`: Real-valued embeddings.
All inputs are finite; a program needn't handle non-finite values.
Results may differ from a plain program's by a relative error of at most 0.0003.
Values may be sent and summed in bfloat16 or wider, within the bound.
A program may use at most 128 MiB of HBM per device.

v0:
```python
import jax
import jax.numpy as jnp
from jax import lax
from jax.sharding import PartitionSpec as P

LOWEST = -1e30


def body(points, prototypes, coarse_duals, active):
    groups = lax.axis_size("pts")
    owners = lax.axis_size("proto")
    blocks, row_count, slice_width = points.shape
    active_width = active.shape[1]
    pair_total = blocks * active_width
    capacity = max(2, 2 * pair_total // groups)
    bucket_cap = 3 * pair_total // (owners + 4)
    slot_count = groups * capacity
    pair_ids = jnp.arange(pair_total, dtype=jnp.int32)
    slot_ids = jnp.arange(slot_count, dtype=jnp.int32)
    targets = active.reshape(pair_total)
    dest_group = targets // owners
    dest_local = targets % owners
    before = (dest_group[:, None] == dest_group[None, :]) & (pair_ids[None, :] < pair_ids[:, None])
    slot_of_pair = dest_group * capacity + jnp.sum(before.astype(jnp.int32), axis=1)
    slot_hits = slot_of_pair[None, :] == slot_ids[:, None]
    filled = jnp.any(slot_hits, axis=1)
    pair_of_slot = jnp.sum(jnp.where(slot_hits, pair_ids[None, :], 0), axis=1)
    block_of_slot = pair_of_slot // active_width
    send_tag = jnp.where(filled, dest_local[pair_of_slot], owners)
    outgoing = jnp.where(filled[:, None, None], points[block_of_slot], jnp.zeros((), points.dtype))
    arrived, arrived_tag = (
        lax.all_to_all(
            outgoing.reshape(groups, capacity, row_count, slice_width),
            "pts",
            split_axis=0,
            concat_axis=0,
            tiled=True,
        ),
        lax.all_to_all(
            send_tag.reshape(groups, capacity), "pts", split_axis=0, concat_axis=0, tiled=True
        ),
    )
    arrived = arrived.reshape(slot_count, row_count, slice_width)
    arrived_tag = arrived_tag.reshape(slot_count)
    occupied = arrived_tag < owners
    earlier_slots = (arrived_tag[None, :] == arrived_tag[:, None]) & (
        slot_ids[None, :] < slot_ids[:, None]
    )
    position = jnp.sum(earlier_slots.astype(jnp.int32), axis=1)
    bucket_code = jnp.where(occupied, arrived_tag * bucket_cap + position, owners * bucket_cap)
    bucket_ids = jnp.arange(owners * bucket_cap, dtype=jnp.int32)
    bucket_match = bucket_code[None, :] == bucket_ids[:, None]
    taken = jnp.any(bucket_match, axis=1)
    slot_of_bucket = jnp.sum(jnp.where(bucket_match, slot_ids[None, :], 0), axis=1)
    sectioned = jnp.where(
        taken[:, None, None], arrived[slot_of_bucket], jnp.zeros((), arrived.dtype)
    )
    resident = lax.all_to_all(
        sectioned.reshape(owners, bucket_cap, row_count, slice_width),
        "proto",
        split_axis=0,
        concat_axis=3,
        tiled=True,
    )
    resident = resident.reshape(bucket_cap, row_count, slice_width * owners)
    my_index = lax.axis_index("proto")
    my_taken = lax.dynamic_slice_in_dim(taken.reshape(owners, bucket_cap), my_index, 1, 0)[0]
    my_slot = lax.dynamic_slice_in_dim(slot_of_bucket.reshape(owners, bucket_cap), my_index, 1, 0)[
        0
    ]
    owned_block = prototypes[0]
    scores = jnp.einsum("hrd,cd->hrc", resident, owned_block, preferred_element_type=jnp.float32)
    shifted = scores + coarse_duals[0][None, None, :]
    row_peak = jnp.max(shifted, axis=2)
    row_mass = jnp.sum(jnp.exp(shifted - row_peak[:, :, None]), axis=2)
    all_peak, all_mass = (
        lax.all_gather(row_peak[None], "proto", axis=0, tiled=True),
        lax.all_gather(row_mass[None], "proto", axis=0, tiled=True),
    )
    all_peak = all_peak.reshape(owners * bucket_cap, row_count)
    all_mass = all_mass.reshape(owners * bucket_cap, row_count)
    lookup = jnp.where(occupied, bucket_code, 0)
    back_peak = jnp.where(occupied[:, None], all_peak[lookup], LOWEST)
    back_mass = jnp.where(occupied[:, None], all_mass[lookup], 0.0)
    got_peak, got_mass = (
        lax.all_to_all(
            back_peak.reshape(groups, capacity, row_count),
            "pts",
            split_axis=0,
            concat_axis=0,
            tiled=True,
        ),
        lax.all_to_all(
            back_mass.reshape(groups, capacity, row_count),
            "pts",
            split_axis=0,
            concat_axis=0,
            tiled=True,
        ),
    )
    pair_peak = got_peak.reshape(slot_count, row_count)[slot_of_pair].reshape(
        blocks, active_width, row_count
    )
    pair_mass = got_mass.reshape(slot_count, row_count)[slot_of_pair].reshape(
        blocks, active_width, row_count
    )
    peak = jnp.max(pair_peak, axis=1)
    mass = jnp.sum(pair_mass * jnp.exp(pair_peak - peak[:, None, :]), axis=1)
    point_duals = -(peak + jnp.log(mass))
    outgoing_duals = jnp.where(filled[:, None], point_duals[block_of_slot], 0.0)
    arrived_duals = lax.all_to_all(
        outgoing_duals.reshape(groups, capacity, row_count),
        "pts",
        split_axis=0,
        concat_axis=0,
        tiled=True,
    )
    my_duals = arrived_duals.reshape(slot_count, row_count)[my_slot]
    rescored = jnp.einsum(
        "hrd,cd->hrc",
        lax.optimization_barrier(resident),
        owned_block,
        preferred_element_type=jnp.float32,
    )
    column_arg = jnp.where(my_taken[:, None, None], rescored + my_duals[:, :, None], LOWEST)
    col_peak = jnp.max(column_arg, axis=(0, 1))
    col_mass = jnp.sum(jnp.exp(column_arg - col_peak[None, None, :]), axis=(0, 1))
    new_duals = -(col_peak + jnp.log(col_mass))
    return (point_duals, new_duals[None, :])


def solution(mesh):
    return jax.shard_map(
        body,
        mesh=mesh,
        in_specs=(
            P("pts", None, "proto"),
            P(("pts", "proto"), None, None),
            P(("pts", "proto"), None),
            P("pts", None),
        ),
        out_specs=(P("pts", None), P(("pts", "proto"), None)),
        check_vma=False,
    )
```

profile of v0, /device:TPU:0, one launch (start us, length us, event | category | flops | bytes accessed | tf_op | source)
XLA Modules:
  0.0 616.0 jit_solution(16729566166568876897)
XLA Ops:
  0.6 0.9 reshape.444
  1.9 1.2 gather_fusion
  3.2 0.7 select_n.191
  3.9 7.4 %all-to-all-start = ((s32[16,1,8]{2,1,0:T(1,128)}), s32[16,1,8]{2,1,0:T(1,128)S(1)}, u32[]{:S(2)}, u32[]{:S(2)}) async-start(s32[16,1,8]{2,1,0:T(1,128)} %bitcast.2), calls=%async_computation | async-start | bytes 16384 | tf_op jit(solution)/shard_map/all_to_all | solution.py:39
  11.3 7.9 %gather_fusion.1 = bf16[128,128,512]{2,1,0:T(8,128)(2,1)} fusion(bf16[8,128,512]{2,1,0:T(8,128)(2,1)S(1)} %copy-done, s32[1024]{0:T(1024)S(1)} %get-tuple-element.14), kind=kCustom, calls=%fused_computation.1 | custom fusion | bytes 33554944 | tf_op jit(solution)/shard_map/gather | solution.py:30
  19.3 14.0 %broadcast_select_fusion = bf16[16,8,128,512]{3,2,1,0:T(8,128)(2,1)} fusion(bf16[16,8,128,512]{3,2,1,0:T(8,128)(2,1)} %bitcast.84, pred[16,8]{1,0:T(8,128)(4,1)S(1)} %broadcast_in_dim.142), kind=kLoop, calls=%fused_computation.9 | loop fusion | flops 8388608 | bytes 33554560 | tf_op jit(solution)/shard_map/jit(_where)/select_n | solution.py:30
  33.3 6.1 all-to-all-start.1
  39.8 0.7 multiply_reduce_fusion
  41.2 294.9 %all-to-all-done.1 = bf16[16,8,128,512]{3,2,1,0:T(8,128)(2,1)} async-done(((bf16[16,8,128,512]{3,2,1,0:T(8,128)(2,1)}), bf16[16,8,128,512]{3,2,1,0:T(8,128)(2,1)}, u32[]{:S(2)}, u32[]{:S(2)}) %all-to-all-start.1) | async-done | bytes 16777248 | tf_op jit(solution)/shard_map/all_to_all | solution.py:32
  336.1 11.3 %gather_fusion.2 = bf16[64,128,512]{2,1,0:T(8,128)(2,1)} fusion(bf16[128,128,512]{2,1,0:T(8,128)(2,1)} %bitcast.6, s32[1024]{0:T(1024)S(1)} %pad_clamp_fusion.3), kind=kCustom, calls=%fused_computation.2 | custom fusion | bytes 16777472 | tf_op jit(solution)/shard_map/gather | solution.py:56
  347.4 7.2 %broadcast_select_fusion.1 = bf16[2,32,128,512]{3,2,1,0:T(8,128)(2,1)} fusion(bf16[2,32,128,512]{3,2,1,0:T(8,128)(2,1)} %bitcast.85, pred[2,32]{1,0:T(4,128)(4,1)S(1)} %broadcast_in_dim.140), kind=kLoop, calls=%fused_computation.13 | loop fusion | flops 4194304 | bytes 16777280 | tf_op jit(solution)/shard_map/jit(_where)/select_n | solution.py:55
  354.6 7.1 %all-to-all-start.2 = ((bf16[2,32,128,512]{3,2,1,0:T(8,128)(2,1)}), bf16[2,32,128,512]{3,2,1,0:T(8,128)(2,1)}, u32[]{:S(2)}, u32[]{:S(2)}) async-start(bf16[2,32,128,512]{3,2,1,0:T(8,128)(2,1)} %broadcast_select_fusion.1), calls=%async_computation.2 | async-start | bytes 16777216 | tf_op jit(solution)/shard_map/all_to_all | solution.py:58
  362.2 93.0 %all-to-all-done.2 = bf16[2,32,128,512]{3,2,1,0:T(8,128)(2,1)} async-done(((bf16[2,32,128,512]{3,2,1,0:T(8,128)(2,1)}), bf16[2,32,128,512]{3,2,1,0:T(8,128)(2,1)}, u32[]{:S(2)}, u32[]{:S(2)}) %all-to-all-start.2) | async-done | bytes 8388640 | tf_op jit(solution)/shard_map/all_to_all | solution.py:58
  455.2 16.4 %copy.20 = bf16[1,32,128,2,512]{4,3,2,1,0:T(2,128)(2,1)} copy(bf16[1,32,128,2,512]{4,2,1,3,0:T(8,128)(2,1)} %bitcast.11) | data formatting | bytes 16777216 | tf_op jit(solution)/shard_map/all_to_all | solution.py:58
  471.6 14.3 %reshape.447 = bf16[32,128,1024]{2,1,0:T(8,128)(2,1)} reshape(bf16[1,32,128,2,512]{4,3,2,1,0:T(2,128)(2,1)} %copy.20) | data formatting | bytes 16777216 | tf_op jit(solution)/shard_map/reshape | solution.py:65
  485.9 7.3 %add_reduce_fusion = (f32[32,128]{1,0:T(8,128)S(1)}, f32[32,128,512]{2,1,0:T(8,128)S(1)}) fusion(f32[512]{0:T(512)S(1)} %bitcast.89, bf16[32,128,1024]{2,1,0:T(8,128)(2,1)} %reshape.447, bf16[1,512,1024]{2,1,0:T(8,128)(2,1)S(1)} %copy-done.5), kind=kOutput, calls=%fused_computation.14 | convolution fusion | flops 4299157504 | bytes 17844224 | tf_op jit(solution)/shard_map/hrd,cd->hrc/dot_general | solution.py:72
  493.2 4.4 all-gather
  497.6 2.0 exponential_reduce_fusion.1
  499.7 4.4 all-gather.1
  504.1 0.6 gather_fusion.5
  504.7 0.6 gather_fusion.3
  505.4 0.7 bitcast_select_fusion.1
  506.1 69.7 %all-to-all-start.3 = ((f32[16,8,128]{2,1,0:T(8,128)}), f32[16,8,128]{2,1,0:T(8,128)S(1)}, u32[]{:S(2)}, u32[]{:S(2)}) async-start(f32[16,8,128]{2,1,0:T(8,128)} %get-tuple-element.5), calls=%async_computation.3 | async-start | bytes 131072 | tf_op jit(solution)/shard_map/all_to_all | solution.py:86
  575.9 6.9 %all-to-all-done.3 = f32[16,8,128]{2,1,0:T(8,128)S(1)} async-done(((f32[16,8,128]{2,1,0:T(8,128)}), f32[16,8,128]{2,1,0:T(8,128)S(1)}, u32[]{:S(2)}, u32[]{:S(2)}) %all-to-all-start.3) | async-done | bytes 65568 | tf_op jit(solution)/shard_map/all_to_all | solution.py:86
  582.8 3.5 all-to-all-start.4
  587.0 6.1 all-to-all-done.4
  593.8 0.6 gather_fusion.7
  594.4 0.7 bitcast_select_fusion
  595.1 3.7 all-to-all-start.5
  598.8 6.6 %all-to-all-done.5 = f32[16,8,128]{2,1,0:T(8,128)S(1)} async-done(((f32[16,8,128]{2,1,0:T(8,128)}), f32[16,8,128]{2,1,0:T(8,128)S(1)}, u32[]{:S(2)}, u32[]{:S(2)}) %all-to-all-start.5) | async-done | bytes 65568 | tf_op jit(solution)/shard_map/all_to_all | solution.py:111
  606.1 7.4 %fusion = (f32[512]{0:T(512)S(1)}, f32[32,128,512]{2,1,0:T(8,128)S(1)}) fusion(f32[32,128]{1,0:T(8,128)S(1)} %gather_fusion.8, pred[32]{0:T(512)(128)(4,1)S(1)} %dynamic-slice_bitcast_fusion, bf16[32,128,1024]{2,1,0:T(8,128)(2,1)} %reshape.447, bf16[1,512,1024]{2,1,0:T(8,128)(2,1)S(1)} %copy-done.5), kind=kOutput, calls=%fused_computation.15 | convolution fusion | flops 4301258240 | bytes 17844256 | tf_op jit(solution)/shard_map/hrd,cd->hrc/dot_general | solution.py:119
  613.5 1.9 exponential_reduce_fusion
  (54 shorter events, 4.7 us)
Async XLA Ops:
  0.6 10.7 %copy-start = (bf16[8,128,512]{2,1,0:T(8,128)(2,1)S(1)}, bf16[8,128,512]{2,1,0:T(8,128)(2,1)}, u32[]{:S(2)}) copy-start(bf16[8,128,512]{2,1,0:T(8,128)(2,1)} %param.4) | copy-start | bytes 3145732
  3.9 29.4 %all-to-all-start = ((s32[16,1,8]{2,1,0:T(1,128)}), s32[16,1,8]{2,1,0:T(1,128)S(1)}, u32[]{:S(2)}, u32[]{:S(2)}) async-start(s32[16,1,8]{2,1,0:T(1,128)} %bitcast.2), calls=%async_computation | async-start | bytes 16384 | tf_op jit(solution)/shard_map/all_to_all | solution.py:39
  33.3 302.8 %all-to-all-start.1 = ((bf16[16,8,128,512]{3,2,1,0:T(8,128)(2,1)}), bf16[16,8,128,512]{3,2,1,0:T(8,128)(2,1)}, u32[]{:S(2)}, u32[]{:S(2)}) async-start(bf16[16,8,128,512]{3,2,1,0:T(8,128)(2,1)} %broadcast_select_fusion), calls=%async_computation.1 | async-start | bytes 33554432 | tf_op jit(solution)/shard_map/all_to_all | solution.py:32
  354.6 7.1 %copy-start.3 = (s32[8,8]{1,0:T(8,128)S(1)}, s32[8,8]{1,0:T(8,128)}, u32[]{:S(2)}) copy-start(s32[8,8]{1,0:T(8,128)} %param.7) | copy-start | bytes 772
  354.6 100.6 %all-to-all-start.2 = ((bf16[2,32,128,512]{3,2,1,0:T(8,128)(2,1)}), bf16[2,32,128,512]{3,2,1,0:T(8,128)(2,1)}, u32[]{:S(2)}, u32[]{:S(2)}) async-start(bf16[2,32,128,512]{3,2,1,0:T(8,128)(2,1)} %broadcast_select_fusion.1), calls=%async_computation.2 | async-start | bytes 16777216 | tf_op jit(solution)/shard_map/all_to_all | solution.py:58
  471.6 14.4 %copy-start.4 = (f32[1,512]{1,0:T(1,128)S(1)}, f32[1,512]{1,0:T(1,128)}, u32[]{:S(2)}) copy-start(f32[1,512]{1,0:T(1,128)} %param.6) | copy-start | bytes 6148
  471.6 14.4 %copy-start.5 = (bf16[1,512,1024]{2,1,0:T(8,128)(2,1)S(1)}, bf16[1,512,1024]{2,1,0:T(8,128)(2,1)}, u32[]{:S(2)}) copy-start(bf16[1,512,1024]{2,1,0:T(8,128)(2,1)} %param.5) | copy-start | bytes 3145732
  506.1 76.6 %all-to-all-start.3 = ((f32[16,8,128]{2,1,0:T(8,128)}), f32[16,8,128]{2,1,0:T(8,128)S(1)}, u32[]{:S(2)}, u32[]{:S(2)}) async-start(f32[16,8,128]{2,1,0:T(8,128)} %get-tuple-element.5), calls=%async_computation.3 | async-start | bytes 131072 | tf_op jit(solution)/shard_map/all_to_all | solution.py:86
  582.8 10.4 %all-to-all-start.4 = ((f32[16,8,128]{2,1,0:T(8,128)}), f32[16,8,128]{2,1,0:T(8,128)S(1)}, u32[]{:S(2)}, u32[]{:S(2)}) async-start(f32[16,8,128]{2,1,0:T(8,128)} %get-tuple-element.4), calls=%async_computation.4 | async-start | bytes 131072 | tf_op jit(solution)/shard_map/all_to_all | solution.py:93
  593.8 19.7 %copy-start.2 = (f32[8,128]{1,0:T(8,128)}, f32[8,128]{1,0:T(8,128)S(1)}, u32[]{:S(2)}) copy-start(f32[8,128]{1,0:T(8,128)S(1)} %add_negate_fusion) | copy-start | bytes 12292
  595.1 10.4 %all-to-all-start.5 = ((f32[16,8,128]{2,1,0:T(8,128)}), f32[16,8,128]{2,1,0:T(8,128)S(1)}, u32[]{:S(2)}, u32[]{:S(2)}) async-start(f32[16,8,128]{2,1,0:T(8,128)} %bitcast_select_fusion), calls=%async_computation.5 | async-start | bytes 131072 | tf_op jit(solution)/shard_map/all_to_all | solution.py:111
  606.1 9.9 %copy-start.1 = (bf16[8,128,512]{2,1,0:T(8,128)(2,1)S(1)}, bf16[8,128,512]{2,1,0:T(8,128)(2,1)}, u32[]{:S(2)}) copy-start(bf16[8,128,512]{2,1,0:T(8,128)(2,1)} %param.4) | copy-start | bytes 3145732
where the time goes:
time: 617 us; the launch traced here: 616 us
  waiting for transfers between devices  408 us (66%)
  starting transfers between devices  97.4 us (16%)
  local copies, waits for them, and re-layouts  57.8 us (9%)
  other arithmetic  28.8 us (5%)
  matrix products  14.7 us (2%)
  blocking collectives  8.83 us (1%)
    all_to_all x1, waiting for transfers between devices, body(): lax.all_to_all(outgoing.reshape(groups, capacity, row_count, slice_width)...  295 us
    all_to_all x1, waiting for transfers between devices, body(): lax.all_to_all(sectioned.reshape(owners, bucket_cap, row_count, slice_wid...  93 us
    all_to_all x1, starting transfers between devices, body(): lax.all_to_all(back_peak.reshape(groups, capacity, row_count), 'pts', spl...  69.7 us
    all_to_all x1, local copies, waits for them, and re-layouts, body(): lax.all_to_all(sectioned.reshape(owners, bucket_cap, row_count, slice_wid...  16.4 us
    reshape x1, local copies, waits for them, and re-layouts, body(): resident = resident.reshape(bucket_cap, row_count, slice_width * owners)  14.3 us
    select_n x1, other arithmetic, body(): jnp.where(filled[:, None, None], points[block_of_slot], jnp.zeros((), poi...  14 us
  transfers between devices with their start and end apart: 6, of which 5 were waited for; matrix products, arithmetic and copies ran while one was open for 4% of the time, Pallas kernels for 0%

commit v1 on v0

--- a/solution.py
+++ b/solution.py
@@ -1,9 +1,29 @@
+import functools
 import jax
 import jax.numpy as jnp
 from jax import lax
 from jax.sharding import PartitionSpec as P
 
 LOWEST = -1e30
+
+
+def _raise_halves(panel, axis_tag):
+    response, oldest = (lax.axis_size(axis_tag), lax.axis_index(axis_tag))
+    local_next = panel.shape[0] // response
+    block_last = list(panel.shape)
+    block_last[0] = local_next
+    k_now = block_last[0]
+    block_last[0] = k_now * response
+    later = jnp.zeros(block_last, panel.dtype)
+    for q in range(response):
+        shaped = lax.dynamic_slice_in_dim(panel, (oldest ^ q) * local_next, local_next, axis=0)
+        if q:
+            shaped = lax.ppermute(shaped, axis_tag, [(ix, ix ^ q) for ix in range(response)])
+        later = lax.dynamic_update_slice_in_dim(later, shaped, (oldest ^ q) * k_now, axis=0)
+    return later
+
+
+trace_pieces_all_by_axis = functools.partial(_raise_halves, axis_tag="pts")
 
 
 def body(points, prototypes, coarse_duals, active):
@@ -29,13 +49,7 @@
     send_tag = jnp.where(filled, dest_local[pair_of_slot], owners)
     outgoing = jnp.where(filled[:, None, None], points[block_of_slot], jnp.zeros((), points.dtype))
     arrived, arrived_tag = (
-        lax.all_to_all(
-            outgoing.reshape(groups, capacity, row_count, slice_width),
-            "pts",
-            split_axis=0,
-            concat_axis=0,
-            tiled=True,
-        ),
+        trace_pieces_all_by_axis(outgoing.reshape(groups, capacity, row_count, slice_width)),
         lax.all_to_all(
             send_tag.reshape(groups, capacity), "pts", split_axis=0, concat_axis=0, tiled=True
         ),

time: 617 us -> 666 us (1.079)
  waiting for transfers between devices: 408 us -> 352 us
  blocking collectives: 8.83 us -> 57.2 us
  local copies, waits for them, and re-layouts: 57.8 us -> 96.5 us
  starting transfers between devices: 97.4 us -> 121 us
    all_to_all x2 -> x0, waiting for transfers between devices: 295 us -> none  [the longest x1 295 us: body(): lax.all_to_all(outgoing.reshape(groups, capacity, row_count, slice_width)...]
    ppermute x0 -> x15, waiting for transfers between devices: none -> 239 us  [_raise_halves(): lax.ppermute(shaped, axis_tag, [(ix, ix ^ q) for ix in range(response)])]
    all_to_all x0 -> x1, blocking collectives: none -> 48.2 us  [body(): lax.all_to_all(send_tag.reshape(groups, capacity), 'pts', split_axis=0, c...]
    dynamic_update_slice x0 -> x15, local copies, waits for them, and re-layouts: none -> 28.4 us  [_raise_halves(): lax.dynamic_update_slice_in_dim(later, shaped, (oldest ^ q) * k_now, axis=0)]
    ppermute x0 -> x15, starting transfers between devices: none -> 18.7 us  [_raise_halves(): lax.ppermute(shaped, axis_tag, [(ix, ix ^ q) for ix in range(response)])]
    all_to_all x1, starting transfers between devices: 69.7 us -> 88.3 us  [body(): lax.all_to_all(back_peak.reshape(groups, capacity, row_count), 'pts', spl...]
    all_to_all x2 -> x0, starting transfers between devices: 13.4 us -> none  [the longest x1 7.36 us: body(): lax.all_to_all(send_tag.reshape(groups, capacity), 'pts', split_axis=0, c...]
  transfers between devices with their start and end apart: 6 -> 19, of which waited for: 5 -> 9; matrix products, arithmetic and copies ran while one was open for 4% -> 5% of each run, Pallas kernels for 0% -> 0%
where the time goes in v1:
time: 666 us; the launch traced here: 665 us
  waiting for transfers between devices  352 us (53%)
  starting transfers between devices  121 us (18%)
  local copies, waits for them, and re-layouts  96.5 us (14%)
  blocking collectives  57.2 us (9%)
  other arithmetic  23.1 us (3%)
  matrix products  14.7 us (2%)
    ppermute x15, waiting for transfers between devices, _raise_halves(): lax.ppermute(shaped, axis_tag, [(ix, ix ^ q) for ix in range(response)])  239 us
    all_to_all x1, waiting for transfers between devices, body(): lax.all_to_all(sectioned.reshape(owners, bucket_cap, row_count, slice_wid...  92.3 us
    all_to_all x1, starting transfers between devices, body(): lax.all_to_all(back_peak.reshape(groups, capacity, row_count), 'pts', spl...  88.3 us
    all_to_all x1, blocking collectives, body(): lax.all_to_all(send_tag.reshape(groups, capacity), 'pts', split_axis=0, c...  48.2 us
    dynamic_update_slice x15, local copies, waits for them, and re-layouts, _raise_halves(): lax.dynamic_update_slice_in_dim(later, shaped, (oldest ^ q) * k_now, axis=0)  28.4 us
    ppermute x15, starting transfers between devices, _raise_halves(): lax.ppermute(shaped, axis_tag, [(ix, ix ^ q) for ix in range(response)])  18.7 us
    all_to_all x1, local copies, waits for them, and re-layouts, body(): lax.all_to_all(sectioned.reshape(owners, bucket_cap, row_count, slice_wid...  16.5 us
    reshape x1, local copies, waits for them, and re-layouts, body(): resident = resident.reshape(bucket_cap, row_count, slice_width * owners)  14.2 us
  transfers between devices with their start and end apart: 19, of which 9 were waited for; matrix products, arithmetic and copies ran while one was open for 5% of the time, Pallas kernels for 0%

profile of v1, /device:TPU:0, one launch (start us, length us, event | category | flops | bytes accessed | tf_op | source)
XLA Modules:
  0.0 665.2 jit_solution(2263288871396586030)
XLA Ops:
  2.2 7.9 %gather_fusion.1 = bf16[128,128,512]{2,1,0:T(8,128)(2,1)} fusion(bf16[8,128,512]{2,1,0:T(8,128)(2,1)S(1)} %copy-done, s32[1024]{0:T(1024)S(1)} %get-tuple-element.30), kind=kCustom, calls=%fused_computation.1 | custom fusion | bytes 33554944 | tf_op jit(solution)/shard_map/gather | solution.py:50
  10.1 8.3 %broadcast_select_fusion = bf16[16,8,128,512]{3,2,1,0:T(8,128)(2,1)S(1)} fusion(bf16[16,8,128,512]{3,2,1,0:T(8,128)(2,1)} %bitcast.86, pred[16,8]{1,0:T(8,128)(4,1)S(1)} %broadcast_in_dim.144), kind=kLoop, calls=%fused_computation.9 | loop fusion | flops 8388608 | bytes 33554560 | tf_op jit(solution)/shard_map/jit(_where)/select_n | solution.py:50
  18.4 5.9 broadcast_in_dim.143
  24.3 4.9 constant_dynamic-slice_fusion.1
  29.8 2.3 collective-permute-start.1
  35.5 48.2 %all_to_all.36 = s32[16,1,8]{2,1,0:T(1,128)S(1)} all-to-all(s32[16,1,8]{2,1,0:T(1,128)S(1)} %bitcast.92), channel_id=1, replica_groups=mesh['pts'=16,'proto'=2] {'pts'}, dimensions={0} | all-to-all | bytes 1024 | tf_op jit(solution)/shard_map/all_to_all | solution.py:53
  88.1 2.7 collective-permute-start.8
  91.6 2.3 constant_dynamic-update-slice_fusion.14
  96.2 58.2 %collective-permute-done.5 = bf16[1,8,128,512]{3,2,1,0:T(8,128)(2,1)} collective-permute-done((bf16[1,8,128,512]{3,2,1,0:T(8,128)(2,1)}, bf16[1,8,128,512]{3,2,1,0:T(8,128)(2,1)}, u32[]{:S(2)}, u32[]{:S(2)}) %collective-permute-start.5) | collective-permute-done | bytes 1048608 | tf_op jit(solution)/shard_map/ppermute | solution.py:21
  156.6 17.8 %collective-permute-done.6 = bf16[1,8,128,512]{3,2,1,0:T(8,128)(2,1)} collective-permute-done((bf16[1,8,128,512]{3,2,1,0:T(8,128)(2,1)}, bf16[1,8,128,512]{3,2,1,0:T(8,128)(2,1)}, u32[]{:S(2)}, u32[]{:S(2)}) %collective-permute-start.6) | collective-permute-done | bytes 1048608 | tf_op jit(solution)/shard_map/ppermute | solution.py:21
  174.4 2.4 collective-permute-start.11
  181.1 2.3 constant_dynamic-update-slice_fusion.10
  183.5 88.5 %collective-permute-done.8 = bf16[1,8,128,512]{3,2,1,0:T(8,128)(2,1)} collective-permute-done((bf16[1,8,128,512]{3,2,1,0:T(8,128)(2,1)}, bf16[1,8,128,512]{3,2,1,0:T(8,128)(2,1)}, u32[]{:S(2)}, u32[]{:S(2)}) %collective-permute-start.8) | collective-permute-done | bytes 1048608 | tf_op jit(solution)/shard_map/ppermute | solution.py:21
  275.5 41.4 %collective-permute-done.9 = bf16[1,8,128,512]{3,2,1,0:T(8,128)(2,1)} collective-permute-done((bf16[1,8,128,512]{3,2,1,0:T(8,128)(2,1)}, bf16[1,8,128,512]{3,2,1,0:T(8,128)(2,1)}, u32[]{:S(2)}, u32[]{:S(2)}) %collective-permute-start.9) | collective-permute-done | bytes 1048608 | tf_op jit(solution)/shard_map/ppermute | solution.py:21
  321.3 2.4 constant_dynamic-update-slice_fusion.7
  328.2 33.5 %collective-permute-done.10 = bf16[1,8,128,512]{3,2,1,0:T(8,128)(2,1)S(1)} collective-permute-done((bf16[1,8,128,512]{3,2,1,0:T(8,128)(2,1)}, bf16[1,8,128,512]{3,2,1,0:T(8,128)(2,1)S(1)}, u32[]{:S(2)}, u32[]{:S(2)}) %collective-permute-start.10) | collective-permute-done | bytes 1048608 | tf_op jit(solution)/shard_map/ppermute | solution.py:21
  367.2 11.3 %gather_fusion.2 = bf16[64,128,512]{2,1,0:T(8,128)(2,1)} fusion(bf16[128,128,512]{2,1,0:T(8,128)(2,1)} %bitcast.87, s32[1024]{0:T(1024)S(1)} %pad_clamp_fusion.3), kind=kCustom, calls=%fused_computation.2 | custom fusion | bytes 16777472 | tf_op jit(solution)/shard_map/gather | solution.py:70
  378.6 7.2 %broadcast_select_fusion.1 = bf16[2,32,128,512]{3,2,1,0:T(8,128)(2,1)} fusion(bf16[2,32,128,512]{3,2,1,0:T(8,128)(2,1)} %bitcast.88, pred[2,32]{1,0:T(4,128)(4,1)S(1)} %broadcast_in_dim.141), kind=kLoop, calls=%fused_computation.13 | loop fusion | flops 4194304 | bytes 16777280 | tf_op jit(solution)/shard_map/jit(_where)/select_n | solution.py:69
  385.8 6.9 %all-to-all-start.1 = ((bf16[2,32,128,512]{3,2,1,0:T(8,128)(2,1)}), bf16[2,32,128,512]{3,2,1,0:T(8,128)(2,1)}, u32[]{:S(2)}, u32[]{:S(2)}) async-start(bf16[2,32,128,512]{3,2,1,0:T(8,128)(2,1)} %broadcast_select_fusion.1), calls=%async_computation.1 | async-start | bytes 16777216 | tf_op jit(solution)/shard_map/all_to_all | solution.py:72
  393.3 92.3 %all-to-all-done.1 = bf16[2,32,128,512]{3,2,1,0:T(8,128)(2,1)} async-done(((bf16[2,32,128,512]{3,2,1,0:T(8,128)(2,1)}), bf16[2,32,128,512]{3,2,1,0:T(8,128)(2,1)}, u32[]{:S(2)}, u32[]{:S(2)}) %all-to-all-start.1) | async-done | bytes 8388640 | tf_op jit(solution)/shard_map/all_to_all | solution.py:72
  485.6 16.5 %copy.20 = bf16[1,32,128,2,512]{4,3,2,1,0:T(2,128)(2,1)} copy(bf16[1,32,128,2,512]{4,2,1,3,0:T(8,128)(2,1)} %bitcast.11) | data formatting | bytes 16777216 | tf_op jit(solution)/shard_map/all_to_all | solution.py:72
  502.1 14.2 %reshape.447 = bf16[32,128,1024]{2,1,0:T(8,128)(2,1)} reshape(bf16[1,32,128,2,512]{4,3,2,1,0:T(2,128)(2,1)} %copy.20) | data formatting | bytes 16777216 | tf_op jit(solution)/shard_map/reshape | solution.py:79
  516.3 7.3 %add_reduce_fusion = (f32[32,128]{1,0:T(8,128)S(1)}, f32[32,128,512]{2,1,0:T(8,128)S(1)}) fusion(f32[512]{0:T(512)S(1)} %bitcast.93, bf16[32,128,1024]{2,1,0:T(8,128)(2,1)} %reshape.447, bf16[1,512,1024]{2,1,0:T(8,128)(2,1)S(1)} %copy-done.5), kind=kOutput, calls=%fused_computation.14 | convolution fusion | flops 4299157504 | bytes 17844224 | tf_op jit(solution)/shard_map/hrd,cd->hrc/dot_general | solution.py:86
  523.6 4.6 all-gather
  530.2 4.4 all-gather.1
  536.7 88.3 %all-to-all-start.2 = ((f32[16,8,128]{2,1,0:T(8,128)}), f32[16,8,128]{2,1,0:T(8,128)S(1)}, u32[]{:S(2)}, u32[]{:S(2)}) async-start(f32[16,8,128]{2,1,0:T(8,128)} %get-tuple-element.21), calls=%async_computation.2 | async-start | bytes 131072 | tf_op jit(solution)/shard_map/all_to_all | solution.py:100
  625.1 6.9 %all-to-all-done.2 = f32[16,8,128]{2,1,0:T(8,128)S(1)} async-done(((f32[16,8,128]{2,1,0:T(8,128)}), f32[16,8,128]{2,1,0:T(8,128)S(1)}, u32[]{:S(2)}, u32[]{:S(2)}) %all-to-all-start.2) | async-done | bytes 65568 | tf_op jit(solution)/shard_map/all_to_all | solution.py:100
  631.9 3.5 all-to-all-start.3
  636.1 6.1 all-to-all-done.3
  644.3 3.5 all-to-all-start.4
  647.8 6.8 %all-to-all-done.4 = f32[16,8,128]{2,1,0:T(8,128)S(1)} async-done(((f32[16,8,128]{2,1,0:T(8,128)}), f32[16,8,128]{2,1,0:T(8,128)S(1)}, u32[]{:S(2)}, u32[]{:S(2)}) %all-to-all-start.4) | async-done | bytes 65568 | tf_op jit(solution)/shard_map/all_to_all | solution.py:125
  655.2 7.4 %fusion = (f32[512]{0:T(512)S(1)}, f32[32,128,512]{2,1,0:T(8,128)S(1)}) fusion(f32[32,128]{1,0:T(8,128)S(1)} %gather_fusion.8, pred[32]{0:T(512)(128)(4,1)S(1)} %fusion.11, bf16[32,128,1024]{2,1,0:T(8,128)(2,1)} %reshape.447, bf16[1,512,1024]{2,1,0:T(8,128)(2,1)S(1)} %copy-done.5), kind=kOutput, calls=%fused_computation.15 | convolution fusion | flops 4301258240 | bytes 17844256 | tf_op jit(solution)/shard_map/hrd,cd->hrc/dot_general | solution.py:133
  (98 shorter events, 47.5 us)
Async XLA Ops:
  0.6 1.5 copy-start
  29.3 56.0 %collective-permute-start = (bf16[1,8,128,512]{3,2,1,0:T(8,128)(2,1)}, bf16[1,8,128,512]{3,2,1,0:T(8,128)(2,1)}, u32[]{:S(2)}, u32[]{:S(2)}) collective-permute-start(bf16[1,8,128,512]{3,2,1,0:T(8,128)(2,1)} %get-tuple-element.18), channel_id=1, source_target_pairs={{0,2},{2,0},{4,6},{6,4},{8,10},{10,8},{12,14},{14,12},{16,18},{18,... | collective-permute-start | bytes 3145736 | tf_op jit(solution)/shard_map/ppermute | solution.py:21
  29.8 56.0 %collective-permute-start.1 = (bf16[1,8,128,512]{3,2,1,0:T(8,128)(2,1)}, bf16[1,8,128,512]{3,2,1,0:T(8,128)(2,1)}, u32[]{:S(2)}, u32[]{:S(2)}) collective-permute-start(bf16[1,8,128,512]{3,2,1,0:T(8,128)(2,1)} %get-tuple-element.17), channel_id=1, source_target_pairs={{0,4},{2,6},{4,0},{6,2},{8,12},{10,14},{12,8},{14,10},{16,20},{18,... | collective-permute-start | bytes 3145736 | tf_op jit(solution)/shard_map/ppermute | solution.py:21
  32.2 55.2 %collective-permute-start.2 = (bf16[1,8,128,512]{3,2,1,0:T(8,128)(2,1)}, bf16[1,8,128,512]{3,2,1,0:T(8,128)(2,1)}, u32[]{:S(2)}, u32[]{:S(2)}) collective-permute-start(bf16[1,8,128,512]{3,2,1,0:T(8,128)(2,1)} %get-tuple-element.16), channel_id=1, source_target_pairs={{0,6},{2,4},{4,2},{6,0},{8,14},{10,12},{12,10},{14,8},{16,22},{18,... | collective-permute-start | bytes 3145736 | tf_op jit(solution)/shard_map/ppermute | solution.py:21
  32.2 55.8 %collective-permute-start.3 = (bf16[1,8,128,512]{3,2,1,0:T(8,128)(2,1)}, bf16[1,8,128,512]{3,2,1,0:T(8,128)(2,1)}, u32[]{:S(2)}, u32[]{:S(2)}) collective-permute-start(bf16[1,8,128,512]{3,2,1,0:T(8,128)(2,1)} %get-tuple-element.15), channel_id=1, source_target_pairs={{0,8},{2,10},{4,12},{6,14},{8,0},{10,2},{12,4},{14,6},{16,24},{18,... | collective-permute-start | bytes 3145736 | tf_op jit(solution)/shard_map/ppermute | solution.py:21
  34.2 56.6 %collective-permute-start.4 = (bf16[1,8,128,512]{3,2,1,0:T(8,128)(2,1)}, bf16[1,8,128,512]{3,2,1,0:T(8,128)(2,1)}, u32[]{:S(2)}, u32[]{:S(2)}) collective-permute-start(bf16[1,8,128,512]{3,2,1,0:T(8,128)(2,1)} %get-tuple-element.14), channel_id=1, source_target_pairs={{0,10},{2,8},{4,14},{6,12},{8,2},{10,0},{12,6},{14,4},{16,26},{18,... | collective-permute-start | bytes 3145736 | tf_op jit(solution)/shard_map/ppermute | solution.py:21
  85.2 69.1 %collective-permute-start.5 = (bf16[1,8,128,512]{3,2,1,0:T(8,128)(2,1)}, bf16[1,8,128,512]{3,2,1,0:T(8,128)(2,1)}, u32[]{:S(2)}, u32[]{:S(2)}) collective-permute-start(bf16[1,8,128,512]{3,2,1,0:T(8,128)(2,1)} %get-tuple-element.13), channel_id=1, source_target_pairs={{0,12},{2,14},{4,8},{6,10},{8,4},{10,6},{12,0},{14,2},{16,28},{18,... | collective-permute-start | bytes 3145736 | tf_op jit(solution)/shard_map/ppermute | solution.py:21
  85.9 88.5 %collective-permute-start.6 = (bf16[1,8,128,512]{3,2,1,0:T(8,128)(2,1)}, bf16[1,8,128,512]{3,2,1,0:T(8,128)(2,1)}, u32[]{:S(2)}, u32[]{:S(2)}) collective-permute-start(bf16[1,8,128,512]{3,2,1,0:T(8,128)(2,1)} %get-tuple-element.12), channel_id=1, source_target_pairs={{0,14},{2,12},{4,10},{6,8},{8,6},{10,4},{12,2},{14,0},{16,30},{18,... | collective-permute-start | bytes 3145736 | tf_op jit(solution)/shard_map/ppermute | solution.py:21
  87.4 91.7 %collective-permute-start.7 = (bf16[1,8,128,512]{3,2,1,0:T(8,128)(2,1)}, bf16[1,8,128,512]{3,2,1,0:T(8,128)(2,1)}, u32[]{:S(2)}, u32[]{:S(2)}) collective-permute-start(bf16[1,8,128,512]{3,2,1,0:T(8,128)(2,1)} %get-tuple-element.11), channel_id=1, source_target_pairs={{0,16},{2,18},{4,20},{6,22},{8,24},{10,26},{12,28},{14,30},{16,0},... | collective-permute-start | bytes 3145736 | tf_op jit(solution)/shard_map/ppermute | solution.py:21
  88.1 183.9 %collective-permute-start.8 = (bf16[1,8,128,512]{3,2,1,0:T(8,128)(2,1)}, bf16[1,8,128,512]{3,2,1,0:T(8,128)(2,1)}, u32[]{:S(2)}, u32[]{:S(2)}) collective-permute-start(bf16[1,8,128,512]{3,2,1,0:T(8,128)(2,1)} %get-tuple-element.10), channel_id=1, source_target_pairs={{0,18},{2,16},{4,22},{6,20},{8,26},{10,24},{12,30},{14,28},{16,2},... | collective-permute-start | bytes 3145736 | tf_op jit(solution)/shard_map/ppermute | solution.py:21
  90.8 226.1 %collective-permute-start.9 = (bf16[1,8,128,512]{3,2,1,0:T(8,128)(2,1)}, bf16[1,8,128,512]{3,2,1,0:T(8,128)(2,1)}, u32[]{:S(2)}, u32[]{:S(2)}) collective-permute-start(bf16[1,8,128,512]{3,2,1,0:T(8,128)(2,1)} %get-tuple-element.9), channel_id=1, source_target_pairs={{0,20},{2,22},{4,16},{6,18},{8,28},{10,30},{12,24},{14,26},{16,4},... | collective-permute-start | bytes 3145736 | tf_op jit(solution)/shard_map/ppermute | solution.py:21
  154.3 207.4 %collective-permute-start.10 = (bf16[1,8,128,512]{3,2,1,0:T(8,128)(2,1)}, bf16[1,8,128,512]{3,2,1,0:T(8,128)(2,1)S(1)}, u32[]{:S(2)}, u32[]{:S(2)}) collective-permute-start(bf16[1,8,128,512]{3,2,1,0:T(8,128)(2,1)} %get-tuple-element.8), channel_id=1, source_target_pairs={{0,22},{2,20},{4,18},{6,16},{8,30},{10,28},{12,26},{14,24},{16,6},... | collective-permute-start | bytes 3145736 | tf_op jit(solution)/shard_map/ppermute | solution.py:21
  174.4 188.4 %collective-permute-start.11 = (bf16[1,8,128,512]{3,2,1,0:T(8,128)(2,1)}, bf16[1,8,128,512]{3,2,1,0:T(8,128)(2,1)S(1)}, u32[]{:S(2)}, u32[]{:S(2)}) collective-permute-start(bf16[1,8,128,512]{3,2,1,0:T(8,128)(2,1)} %get-tuple-element.7), channel_id=1, source_target_pairs={{0,24},{2,26},{4,28},{6,30},{8,16},{10,18},{12,20},{14,22},{16,8},... | collective-permute-start | bytes 3145736 | tf_op jit(solution)/shard_map/ppermute | solution.py:21
  179.0 184.9 %collective-permute-start.12 = (bf16[1,8,128,512]{3,2,1,0:T(8,128)(2,1)S(1)}, bf16[1,8,128,512]{3,2,1,0:T(8,128)(2,1)S(1)}, u32[]{:S(2)}, u32[]{:S(2)}) collective-permute-start(bf16[1,8,128,512]{3,2,1,0:T(8,128)(2,1)S(1)} %get-tuple-element.6), channel_id=1, source_target_pairs={{0,26},{2,24},{4,30},{6,28},{8,18},{10,16},{12,22},{14,20},{16,10}... | collective-permute-start | bytes 3145736 | tf_op jit(solution)/shard_map/ppermute | solution.py:21
  272.0 93.1 %collective-permute-start.13 = (bf16[1,8,128,512]{3,2,1,0:T(8,128)(2,1)S(1)}, bf16[1,8,128,512]{3,2,1,0:T(8,128)(2,1)S(1)}, u32[]{:S(2)}, u32[]{:S(2)}) collective-permute-start(bf16[1,8,128,512]{3,2,1,0:T(8,128)(2,1)S(1)} %get-tuple-element.5), channel_id=1, source_target_pairs={{0,28},{2,30},{4,24},{6,26},{8,20},{10,22},{12,16},{14,18},{16,12}... | collective-permute-start | bytes 3145736 | tf_op jit(solution)/shard_map/ppermute | solution.py:21
  316.9 49.2 %collective-permute-start.14 = (bf16[1,8,128,512]{3,2,1,0:T(8,128)(2,1)S(1)}, bf16[1,8,128,512]{3,2,1,0:T(8,128)(2,1)S(1)}, u32[]{:S(2)}, u32[]{:S(2)}) collective-permute-start(bf16[1,8,128,512]{3,2,1,0:T(8,128)(2,1)S(1)} %get-tuple-element.4), channel_id=1, source_target_pairs={{0,30},{2,28},{4,26},{6,24},{8,22},{10,20},{12,18},{14,16},{16,14}... | collective-permute-start | bytes 3145736 | tf_op jit(solution)/shard_map/ppermute | solution.py:21
  378.6 14.2 %copy-start.3 = (s32[8,8]{1,0:T(8,128)S(1)}, s32[8,8]{1,0:T(8,128)}, u32[]{:S(2)}) copy-start(s32[8,8]{1,0:T(8,128)} %param.7) | copy-start | bytes 772
  385.8 99.8 %all-to-all-start.1 = ((bf16[2,32,128,512]{3,2,1,0:T(8,128)(2,1)}), bf16[2,32,128,512]{3,2,1,0:T(8,128)(2,1)}, u32[]{:S(2)}, u32[]{:S(2)}) async-start(bf16[2,32,128,512]{3,2,1,0:T(8,128)(2,1)} %broadcast_select_fusion.1), calls=%async_computation.1 | async-start | bytes 16777216 | tf_op jit(solution)/shard_map/all_to_all | solution.py:72
  485.6 30.7 %copy-start.4 = (f32[1,512]{1,0:T(1,128)S(1)}, f32[1,512]{1,0:T(1,128)}, u32[]{:S(2)}) copy-start(f32[1,512]{1,0:T(1,128)} %param.6) | copy-start | bytes 6148
  485.6 30.7 %copy-start.5 = (bf16[1,512,1024]{2,1,0:T(8,128)(2,1)S(1)}, bf16[1,512,1024]{2,1,0:T(8,128)(2,1)}, u32[]{:S(2)}) copy-start(bf16[1,512,1024]{2,1,0:T(8,128)(2,1)} %param.5) | copy-start | bytes 3145732
  536.7 95.2 %all-to-all-start.2 = ((f32[16,8,128]{2,1,0:T(8,128)}), f32[16,8,128]{2,1,0:T(8,128)S(1)}, u32[]{:S(2)}, u32[]{:S(2)}) async-start(f32[16,8,128]{2,1,0:T(8,128)} %get-tuple-element.21), calls=%async_computation.2 | async-start | bytes 131072 | tf_op jit(solution)/shard_map/all_to_all | solution.py:100
  631.9 10.4 %all-to-all-start.3 = ((f32[16,8,128]{2,1,0:T(8,128)}), f32[16,8,128]{2,1,0:T(8,128)S(1)}, u32[]{:S(2)}, u32[]{:S(2)}) async-start(f32[16,8,128]{2,1,0:T(8,128)} %get-tuple-element.20), calls=%async_computation.3 | async-start | bytes 131072 | tf_op jit(solution)/shard_map/all_to_all | solution.py:107
  642.9 19.8 %copy-start.2 = (f32[8,128]{1,0:T(8,128)}, f32[8,128]{1,0:T(8,128)S(1)}, u32[]{:S(2)}) copy-start(f32[8,128]{1,0:T(8,128)S(1)} %add_negate_fusion) | copy-start | bytes 12292
  644.3 10.4 %all-to-all-start.4 = ((f32[16,8,128]{2,1,0:T(8,128)}), f32[16,8,128]{2,1,0:T(8,128)S(1)}, u32[]{:S(2)}, u32[]{:S(2)}) async-start(f32[16,8,128]{2,1,0:T(8,128)} %bitcast_select_fusion), calls=%async_computation.4 | async-start | bytes 131072 | tf_op jit(solution)/shard_map/all_to_all | solution.py:125
  655.2 9.9 %copy-start.1 = (bf16[8,128,512]{2,1,0:T(8,128)(2,1)S(1)}, bf16[8,128,512]{2,1,0:T(8,128)(2,1)}, u32[]{:S(2)}) copy-start(bf16[8,128,512]{2,1,0:T(8,128)(2,1)} %param.4) | copy-start | bytes 3145732
